TPU v7x, 32 devices: a whole 2x2x4 slice. The times are simulated.
32 devices in a mesh: spot: 4 (over x, core), cell: 8 (over z, y).
Axes of the slice: x: 2, y: 2, z: 4, core: 2. Of those that a mesh axis runs over, the one named last changes fastest.
Arguments:
- logits: float32 [4096, 4096], P('cell', 'spot'), may hold values from -6 to 6
- expression: float32 [4096, 2048], P('cell', 'spot'), may hold values from 0.05 to 5
- spatial: float32 [2048, 4096], P('cell', 'spot'), may hold values from 0.05 to 5
- density: float32 [4096], P('spot'), may hold values from 0.2 to 5
- slide_ids: int32 [4096], replicated, may hold values from 0 to 2, as said below
- spot_valid: int32 [4096], replicated, may hold values 0 or 1
- neighbours: int32 [4096, 6], P('spot'), may hold values from -1 to 4095, as said below
Outputs:
- gene_loss: float32 [], replicated
- spot_loss: float32 [], replicated
- density_loss: float32 [], replicated
- grad_logits: float32 [4096, 4096], P('cell', 'spot')
- grad_expr: float32 [4096, 2048], P('cell', 'spot')
- rms_weights: float32 [], replicated
- rms_pred: float32 [], replicated
- rms_smooth: float32 [], replicated
Inputs may be any that keep to these rules, and one draw needn't show every extreme that they name: `slide_ids`: slide ids never fall along the spots, and each of the 3 slides holds whole grid rows of 64 spots. `neighbours`: spots lie row by row on a hexagonal grid with 64 spots a row, odd rows shifted; every listed neighbour is an adjacent grid spot, at most 65 away in index.
All inputs are finite; a program needn't handle non-finite values.
Results may differ from a plain program's by a relative error of at most 0.0003.
Values sent between devices are 32-bit elements; how exact they have to be, the bound alone decides.
No kernel may reach another device: no remote copies, remote signals or barrier semaphores. Data moves between devices by JAX's collectives and lax.ppermute only.
A program may use at most 128 MiB of HBM per device.

v0:
```python
import jax
import jax.numpy as jnp
from jax import lax
from jax.sharding import PartitionSpec as P

GENES = 2048
ROW = 64
SLIDES = 3
epsilon = 1e-06
highest = lax.Precision.HIGHEST


def padded_2(shard, sides, width):
    for axis, dim in sides:
        peers, length = (lax.axis_size(axis), shard.shape[dim])
        up = [(i, (i + 1) % peers) for i in range(peers - 1)]
        down = [(j, i) for i, j in up]
        last = lax.slice_in_dim(shard, length - width, length, axis=dim)
        first = lax.slice_in_dim(shard, 0, width, axis=dim)
        before = lax.ppermute(last, axis, up)
        after = lax.ppermute(first, axis, down)
        shard = jnp.concatenate([before, shard, after], axis=dim)
    return shard


def passed_along(block, axis, distance):
    devices = range(lax.axis_size(axis))
    route = [(i - distance, i) for i in devices if i - distance in devices]
    return lax.ppermute(block, axis, route)


def shards(logits, expression, spatial, density, slide_ids, spot_valid, neighbours):
    local_cells, local_spots = logits.shape
    local_genes = spatial.shape[0]
    total_cells = local_cells * lax.axis_size("cell")
    total_spots = local_spots * lax.axis_size("spot")
    margin = ROW + 1
    offset = lax.axis_index("spot") * local_spots
    valid_all = spot_valid.astype(jnp.float32)
    nvalid = jnp.sum(valid_all)
    valid_here = lax.dynamic_slice_in_dim(valid_all, offset, local_spots)
    slide_here = lax.dynamic_slice_in_dim(slide_ids, offset, local_spots)
    clamped = jnp.maximum(neighbours, 0)
    linked = (
        (neighbours >= 0) & (spot_valid[clamped] == 1) & (slide_ids[clamped] == slide_here[:, None])
    ).astype(jnp.float32)
    counts = 1.0 + jnp.sum(linked, axis=1)
    position = jnp.clip(clamped - offset + margin, 0, local_spots + 2 * margin - 1)
    members = (slide_here[:, None] == jnp.arange(SLIDES, dtype=jnp.int32)[None, :]).astype(
        jnp.float32
    )
    local_max = jnp.max(logits, axis=0)
    column_max = lax.pmax(local_max, "cell")
    raised = jnp.exp(logits - column_max)
    column_sum = lax.psum(jnp.sum(raised, axis=0), "cell")
    mapping = raised / column_sum
    genes_all = lax.all_gather(expression, "spot", axis=1, tiled=True)
    columns = genes_all
    predicted = lax.psum_scatter(
        lax.dot_general(columns, mapping, (((0,), (0,)), ((), ())), precision=highest),
        "cell",
        scatter_dimension=0,
        tiled=True,
    )
    padded = padded_2(predicted, (("spot", 1),), margin)
    summed = predicted
    for k in range(6):
        summed = summed + linked[:, k][None, :] * jnp.take(padded, position[:, k], axis=1)
    smoothed = summed / counts[None, :]
    spot_inner, spot_own, spot_target, row_sums = lax.psum(
        (
            jnp.sum(smoothed * spatial, axis=0),
            jnp.sum(smoothed * smoothed, axis=0),
            jnp.sum(spatial * spatial, axis=0),
            jnp.sum(predicted, axis=0),
        ),
        "cell",
    )
    weighted = valid_here[None, :]
    gene_inner, gene_own, gene_target, row_tot, target_tot = lax.psum(
        (
            jnp.sum(weighted * smoothed * spatial, axis=1),
            jnp.sum(weighted * smoothed * smoothed, axis=1),
            jnp.sum(weighted * spatial * spatial, axis=1),
            jnp.sum(members * (valid_here * row_sums)[:, None], axis=0),
            jnp.sum(members * (valid_here * density)[:, None], axis=0),
        ),
        "spot",
    )
    gene_scale = lax.rsqrt((gene_own + epsilon) * (gene_target + epsilon))
    cos_gene = gene_inner * gene_scale
    spot_scale = lax.rsqrt((spot_own + epsilon) * (spot_target + epsilon))
    cos_spot = spot_inner * spot_scale
    target = density / jnp.sum(members * target_tot[None, :], axis=1)
    slide_rows = jnp.sum(members * row_tot[None, :], axis=1)
    predicted_share = row_sums / slide_rows
    kl_terms = valid_here * target * (jnp.log(target) - jnp.log(predicted_share))
    grad_smooth = (
        -total_cells
        * weighted
        * (spatial - (gene_inner / (gene_own + epsilon))[:, None] * smoothed)
        * gene_scale[:, None]
    )
    grad_smooth = (
        grad_smooth
        - total_cells
        * total_spots
        / nvalid
        * weighted
        * (spatial - (spot_inner / (spot_own + epsilon))[None, :] * smoothed)
        * spot_scale[None, :]
    )
    spread_in = grad_smooth / counts[None, :]
    spread = jnp.zeros((local_genes, local_spots + 2 * margin), jnp.float32)
    for k in range(6):
        spread = spread.at[:, position[:, k]].add(linked[:, k][None, :] * spread_in)
    grad_pred = spread_in + spread[:, margin : margin + local_spots]
    from_next = passed_along(spread[:, :margin], "spot", -1)
    from_prev = passed_along(spread[:, margin + local_spots :], "spot", 1)
    grad_pred = grad_pred.at[:, local_spots - margin :].add(from_next)
    grad_pred = grad_pred.at[:, :margin].add(from_prev)
    grad_pred = (
        grad_pred
        + (total_cells * total_spots * valid_here * (1.0 / slide_rows - target / row_sums))[None, :]
    )
    shard_rows = lax.all_gather(grad_pred, "cell", axis=0, tiled=True)
    columns = genes_all
    grad_map = jnp.dot(columns, shard_rows, precision=highest)
    block_grad = lax.dot_general(mapping, shard_rows, (((1,), (1,)), ((), ())), precision=highest)
    grad_wide = block_grad
    grad_map, grad_wide = (grad_map, grad_wide)
    column_dot = lax.psum(jnp.sum(mapping * grad_map, axis=0), "cell")
    grad_logits = mapping * (grad_map - column_dot[None, :])
    grad_expr = lax.psum_scatter(grad_wide, "spot", scatter_dimension=1, tiled=True)
    first_spot = (lax.axis_index("spot") == 0).astype(jnp.float32)
    first_cell = (lax.axis_index("cell") == 0).astype(jnp.float32)
    totals = lax.psum(
        (
            first_spot * jnp.sum(cos_gene),
            first_cell * jnp.sum(valid_here * cos_spot),
            first_cell * jnp.sum(kl_terms),
            jnp.sum(mapping * mapping * weighted),
            jnp.sum(weighted * predicted * predicted),
            jnp.sum(weighted * smoothed * smoothed),
        ),
        ("spot", "cell"),
    )
    gene_loss = 1.0 - totals[0] / GENES
    spot_loss = 1.0 - totals[1] / nvalid
    density_loss = totals[2]
    rms_weights = total_cells * jnp.sqrt(totals[3] / (total_cells * nvalid))
    rms_pred = jnp.sqrt(totals[4] / (GENES * nvalid))
    rms_smooth = jnp.sqrt(totals[5] / (GENES * nvalid))
    return (
        gene_loss,
        spot_loss,
        density_loss,
        grad_logits,
        grad_expr,
        rms_weights,
        rms_pred,
        rms_smooth,
    )


def solution(mesh):
    placed = (
        P("cell", "spot"),
        P("cell", "spot"),
        P("cell", "spot"),
        P("spot"),
        P(),
        P(),
        P("spot", None),
    )
    return jax.shard_map(
        shards,
        mesh=mesh,
        in_specs=placed,
        out_specs=(P(), P(), P(), P("cell", "spot"), P("cell", "spot"), P(), P(), P()),
        check_vma=False,
    )
```

profile of v0, /device:TPU:0, one launch (start us, length us, event | category | flops | bytes accessed | tf_op | source)
XLA Modules:
  0.0 603.6 jit_solution(575941561613599674)
XLA Ops:
  9.7 23.2 %pmax.7 = f32[1024]{0:T(1024)S(1)} all-reduce(f32[1024]{0:T(1024)S(1)} %reduce_max.9), channel_id=1, replica_groups=mesh['spot'=4,'cell'=8] {'cell'}, use_global_device_ids=true, to_apply=%region_1.0 | all-reduce | flops 1024 | bytes 8192 | tf_op jit(solution)/shard_map/pmax | solution.py:53
  33.2 17.1 %psum.119 = f32[1024]{0:T(1024)S(1)} all-reduce(f32[1024]{0:T(1024)S(1)} %fusion.3), channel_id=1, replica_groups=mesh['spot'=4,'cell'=8] {'cell'}, use_global_device_ids=true, to_apply=%region_3.4 | all-reduce | flops 1024 | bytes 8192 | tf_op jit(solution)/shard_map/psum | solution.py:55
  50.4 17.3 %convolution_bitcast_fusion = f32[2048,1024]{0,1:T(8,128)} fusion(f32[512,2048]{1,0:T(8,128)} %all-gather.3.cloned.1.call-done, f32[512,1024]{1,0:T(8,128)S(1)} %copy-done.3, f32[1024]{0:T(1024)S(1)} %psum.119, f32[1024]{0:T(1024)S(1)} %pmax.7), kind=kOutput, calls=%fused_computation.14 | convolution fusion | flops 12885950464 | bytes 14688256 | tf_op jit(solution)/shard_map/dot_general | solution.py:60
  72.3 60.4 %gather_fusion = s32[6144]{0:T(1024)} fusion(s32[4096]{0:T(1024)S(1)} %copy-done, s32[6144]{0:T(1024)S(1)} %broadcast_clamp_fusion), kind=kCustom, calls=%fused_computation.6 | custom fusion | bytes 73728 | tf_op jit(solution)/shard_map/gather | solution.py:45
  132.7 28.4 %gather_fusion.1 = s32[6144]{0:T(1024)S(1)} fusion(s32[4096]{0:T(1024)} %param.17, s32[6144]{0:T(1024)S(1)} %broadcast_clamp_fusion), kind=kCustom, calls=%fused_computation.7 | custom fusion | bytes 73728 | tf_op jit(solution)/shard_map/gather | solution.py:45
  169.7 44.7 %reduce-scatter.3.cloned.1.call-done = f32[256,1024]{0,1:T(8,128)} async-done(((f32[2048,1024]{0,1:T(8,128)}), f32[256,1024]{0,1:T(8,128)}) %reduce-scatter.3.cloned.1.call-update) | async-done | bytes 1048592 | tf_op jit(solution)/shard_map/reduce_scatter | solution.py:59
  224.7 4.7 gather_fusion.7
  229.4 4.7 gather_fusion.6
  234.1 4.7 gather_fusion.5
  238.7 4.7 gather_fusion.4
  252.7 7.7 %multiply_reduce_fusion.3 = (f32[1024]{0:T(1024)S(1)}, f32[256]{0:T(256)S(1)}, f32[]{:T(128)}, f32[256]{0:T(256)S(1)}, f32[256]{0:T(256)S(1)}, /*index=5*/f32[10...) fusion(f32[256,1024]{0,1:T(8,128)S(1)} %copy-done.6, f32[1024]{0:T(1024)S(1)} %get-tuple-element.85, ...), kind=kLoop, calls=%fused_computation.71 | loop fusion | flops 9433342 | bytes 9491464 | tf_op jit(solution)/shard_map/reduce_sum | solution.py:72
  260.4 35.2 %all-reduce.1 = (f32[1024]{0:T(1024)S(1)}, f32[1024]{0:T(1024)S(1)}, f32[1024]{0:T(1024)S(1)}, f32[1024]{0:T(1024)S(1)}) all-reduce(f32[1024]{0:T(1024)S(1)} %get-tuple-element.61, f32[1024]{0:T(1024)S(1)} %get-tuple-element.35, f32[1024]{0:T(1024)S(1)} %multiply_reduce_fusion.1, ...), channel_id=1, replica_groups=mesh['spot'=4,'cell'=8] {'cell'}, use_global_device_ids=true, to_apply=%region_27.29 | all-reduce | flops 4096 | bytes 32768 | tf_op jit(solution)/shard_map/psum | solution.py:70
  295.8 6.6 %all-reduce.2 = (f32[256]{0:T(256)S(1)}, f32[256]{0:T(256)S(1)}, f32[256]{0:T(256)S(1)}, f32[3]{0:T(128)S(1)}, f32[3]{0:T(128)S(1)}) all-reduce(f32[256]{0:T(256)S(1)} %get-tuple-element.36, f32[256]{0:T(256)S(1)} %get-tuple-element.38, f32[256]{0:T(256)S(1)} %get-tuple-element.39, ...), channel_id=1, replica_groups=mesh['spot'=4,'cell'=8] {'spot'}, use_global_device_ids=true, to_apply=%region_7.9 | all-reduce | flops 774 | bytes 6192 | tf_op jit(solution)/shard_map/psum | solution.py:80
  304.6 6.8 %scatter_custom_fusion = f32[256,1154]{0,1:T(8,128)S(1)} fusion(s32[1024]{0:T(1024)S(1)} %get-tuple-element.44, f32[256,1024]{0,1:T(8,128)S(1)} %subtract_divide_fusion, f32[]{:T(128)} %constant.106.clone.1, f32[1024]{0:T(1024)S(1)} %get-tuple-element.55), kind=kCustom, calls=%fused_computation.47 | custom fusion | flops 524288 | bytes 2234372 | tf_op jit(solution)/shard_map/scatter-add | solution.py:116
  311.5 7.0 %scatter_custom_fusion.1 = f32[256,1154]{0,1:T(8,128)S(1)} fusion(f32[256,1154]{0,1:T(8,128)S(1)} %scatter_custom_fusion, s32[1024]{0:T(1024)S(1)} %get-tuple-element.45, f32[256,1024]{0,1:T(8,128)S(1)} %subtract_divide_fusion, f32[1024]{0:T(1024)S(1)} %get-tuple-element.60), kind=kCustom, calls=%fused_computation.45 | custom fusion | flops 524288 | bytes 2234368 | tf_op jit(solution)/shard_map/scatter-add | solution.py:116
  318.5 7.1 %scatter_custom_fusion.2 = f32[256,1154]{0,1:T(8,128)S(1)} fusion(f32[256,1154]{0,1:T(8,128)S(1)} %scatter_custom_fusion.1, s32[1024]{0:T(1024)S(1)} %get-tuple-element.46, f32[256,1024]{0,1:T(8,128)S(1)} %subtract_divide_fusion, f32[1024]{0:T(1024)S(1)} %get-tuple-element.59), kind=kCustom, calls=%fused_computation.43 | custom fusion | flops 524288 | bytes 2234368 | tf_op jit(solution)/shard_map/scatter-add | solution.py:116
  325.5 7.1 %scatter_custom_fusion.3 = f32[256,1154]{0,1:T(8,128)S(1)} fusion(f32[256,1154]{0,1:T(8,128)S(1)} %scatter_custom_fusion.2, s32[1024]{0:T(1024)S(1)} %get-tuple-element.47, f32[256,1024]{0,1:T(8,128)S(1)} %subtract_divide_fusion, f32[1024]{0:T(1024)S(1)} %get-tuple-element.58), kind=kCustom, calls=%fused_computation.41 | custom fusion | flops 524288 | bytes 2234368 | tf_op jit(solution)/shard_map/scatter-add | solution.py:116
  332.6 7.4 %scatter_custom_fusion.4 = f32[256,1154]{0,1:T(8,128)S(1)} fusion(f32[256,1154]{0,1:T(8,128)S(1)} %scatter_custom_fusion.3, s32[1024]{0:T(1024)S(1)} %get-tuple-element.48, f32[256,1024]{0,1:T(8,128)S(1)} %subtract_divide_fusion, f32[1024]{0:T(1024)S(1)} %get-tuple-element.57), kind=kCustom, calls=%fused_computation.39 | custom fusion | flops 524288 | bytes 2234368 | tf_op jit(solution)/shard_map/scatter-add | solution.py:116
  340.0 7.0 %scatter_custom_fusion.5 = f32[256,1154]{0,1:T(8,128)S(1)} fusion(f32[256,1154]{0,1:T(8,128)S(1)} %scatter_custom_fusion.4, s32[1024]{0:T(1024)S(1)} %get-tuple-element.43, f32[256,1024]{0,1:T(8,128)S(1)} %subtract_divide_fusion, f32[1024]{0:T(1024)S(1)} %get-tuple-element.56), kind=kCustom, calls=%fused_computation.37 | custom fusion | flops 524288 | bytes 2234368 | tf_op jit(solution)/shard_map/scatter-add | solution.py:116
  357.2 125.2 %all-gather.5.cloned.1.call-done = f32[2048,1024]{0,1:T(8,128)} async-done(((f32[256,1024]{0,1:T(8,128)}), f32[2048,1024]{0,1:T(8,128)}) %all-gather.5.cloned.1.call-update) | async-done | bytes 8388624 | tf_op jit(solution)/shard_map/all_gather | solution.py:126
  482.4 17.5 %fusion.53 = f32[512,2048]{1,0:T(8,128)} fusion(f32[2048,1024]{0,1:T(8,128)} %all-gather.5.cloned.1.call-done, f32[512,1024]{1,0:T(8,128)S(1)} %copy-done.4, f32[1024]{0:T(1024)S(1)} %copy-done.17, f32[1024]{0:T(1024)S(1)} %copy-done.14), kind=kOutput, calls=%fused_computation.144 | convolution fusion | flops 12885950464 | bytes 14688256 | tf_op jit(solution)/shard_map/dot_general | solution.py:129
  503.2 19.9 %multiply_reduce_fusion = (f32[]{:T(128)}, f32[1024]{0:T(1024)S(1)}, f32[1024,512]{0,1:T(8,128)}) fusion(f32[1024]{0:T(1024)S(1)} %get-tuple-element.85, f32[1024]{0:T(1024)S(1)} %copy-done.17, f32[512,1024]{1,0:T(8,128)S(1)} %copy-done.4, f32[1024]{0:T(1024)S(1)} %copy-done.14, f32[2048,1024]{0,1:T(8,128)} %all-gather.5.cloned.1.call-done, ...), kind=kOutput, calls=%fused_computation.19 | convolution fusion | flops 12888570880 | bytes 16793604 | tf_op jit(solution)/shard_map/dot_general | solution.py:128
  523.0 39.3 %all-reduce = (f32[]{:T(128)}, f32[]{:T(128)}, f32[]{:T(128)}, f32[]{:T(128)}, f32[]{:T(128)}, /*index=5*/f32[]{:T(128)}) all-reduce(f32[]{:T(128)S(6)} %mul.342, f32[]{:T(128)S(6)} %mul.349, f32[]{:T(128)S(6)} %mul.362, f32[]{:T(128)} %get-tuple-element.33, ...), channel_id=1, replica_groups=mesh['spot'=4,'cell'=8] {'spot','cell'}, use_global_device_ids=true, to_apply=%region_13.15 | all-reduce | flops 6 | bytes 48 | tf_op jit(solution)/shard_map/psum | solution.py:137
  566.4 21.4 %psum.132 = f32[1024]{0:T(1024)S(1)} all-reduce(f32[1024]{0:T(1024)S(1)} %get-tuple-element.34), channel_id=1, replica_groups=mesh['spot'=4,'cell'=8] {'cell'}, use_global_device_ids=true, to_apply=%region_41.43 | all-reduce | flops 1024 | bytes 8192 | tf_op jit(solution)/shard_map/psum | solution.py:132
  (100 shorter events, 50.8 us)
Async XLA Ops:
  7.2 25.7 %copy-start.3 = (f32[512,1024]{1,0:T(8,128)S(1)}, f32[512,1024]{1,0:T(8,128)}, u32[]{:S(2)}) copy-start(f32[512,1024]{1,0:T(8,128)} %param.13) | copy-start | bytes 6291460
  7.2 43.2 %all-gather.3.cloned.1.call-start = ((), (), s32[]{:S(2)}) async-start(), calls=%async_computation.2 | async-start | bytes 5242880 | tf_op jit(solution)/shard_map/all_gather | solution.py:57
  7.9 206.5 %reduce-scatter.3.cloned.1.call-start = ((), (), s32[]{:S(2)}) async-start(), calls=%async_computation.3 | async-start | bytes 9437184 | tf_op jit(solution)/shard_map/reduce_scatter | solution.py:59
  32.9 34.8 %copy-start.13 = (f32[1024]{0:T(1024)}, f32[1024]{0:T(1024)S(1)}, u32[]{:S(2)}) copy-start(f32[1024]{0:T(1024)S(1)} %pmax.7) | copy-start | bytes 12292
  50.3 17.3 %copy-start.16 = (f32[1024]{0:T(1024)}, f32[1024]{0:T(1024)S(1)}, u32[]{:S(2)}) copy-start(f32[1024]{0:T(1024)S(1)} %psum.119) | copy-start | bytes 12292
  67.7 2.5 copy-start
  67.7 3.1 copy-start.11
  67.7 414.7 %all-gather.5.cloned.1.call-start = ((), (), s32[]{:S(2)}) async-start(), calls=%async_computation.4 | async-start | bytes 9437184 | tf_op jit(solution)/shard_map/all_gather | solution.py:126
  132.7 29.6 %copy-start.12 = (s32[1024,6]{0,1:T(8,128)S(1)}, s32[1024,6]{0,1:T(8,128)}, u32[]{:S(2)}) copy-start(s32[1024,6]{0,1:T(8,128)} %param.19) | copy-start | bytes 73732
  132.7 29.9 %copy-start.5 = (s32[6144]{0:T(1024)S(1)}, s32[6144]{0:T(1024)}, u32[]{:S(2)}) copy-start(s32[6144]{0:T(1024)} %gather_fusion) | copy-start | bytes 73732
  132.7 30.5 %copy-start.1 = (s32[4096]{0:T(1024)S(1)}, s32[4096]{0:T(1024)}, u32[]{:S(2)}) copy-start(s32[4096]{0:T(1024)} %param.18) | copy-start | bytes 49156
  132.7 32.4 %copy-start.10 = (f32[256,1024]{1,0:T(8,128)S(1)}, f32[256,1024]{1,0:T(8,128)}, u32[]{:S(2)}) copy-start(f32[256,1024]{1,0:T(8,128)} %param.15) | copy-start | bytes 3145732
  165.2 2.0 copy-start.2
  215.3 3.5 collective-permute-start
  216.8 4.7 collective-permute-start.1
  248.1 4.7 copy-start.6
  248.1 4.7 copy-start.7
  252.7 42.9 %copy-start.15 = (f32[1024]{0:T(1024)S(1)}, f32[1024]{0:T(1024)}, u32[]{:S(2)}) copy-start(f32[1024]{0:T(1024)} %param.16) | copy-start | bytes 12292
  348.0 5.9 collective-permute-start.2
  350.6 131.8 %copy-start.4 = (f32[512,1024]{1,0:T(8,128)S(1)}, f32[512,1024]{1,0:T(8,128)}, u32[]{:S(2)}) copy-start(f32[512,1024]{1,0:T(8,128)} %param.13) | copy-start | bytes 6291460
  350.7 131.8 %copy-start.14 = (f32[1024]{0:T(1024)S(1)}, f32[1024]{0:T(1024)}, u32[]{:S(2)}) copy-start(f32[1024]{0:T(1024)} %copy-done.13) | copy-start | bytes 12292
  350.7 131.8 %copy-start.17 = (f32[1024]{0:T(1024)S(1)}, f32[1024]{0:T(1024)}, u32[]{:S(2)}) copy-start(f32[1024]{0:T(1024)} %copy-done.16) | copy-start | bytes 12292
  350.7 4.1 collective-permute-start.3
  357.2 234.1 %reduce-scatter.5.cloned.1.call-start = ((), (), s32[]{:S(2)}) async-start(), calls=%async_computation.5 | async-start | bytes 5242880 | tf_op jit(solution)/shard_map/reduce_scatter | solution.py:134
  (2 other events, 2.2 us)
Sparse Core Ops, SparseCore 0:
  9.5 37.1 all-gather.2
  67.8 146.5 reduce-scatter.2
  357.3 125.0 all-gather.4
  500.0 43.2 reduce-scatter.4
where the time goes:
time: 610 us; the launch traced here: 604 us
  waiting for transfers between devices  174 us (29%)
  blocking collectives  143 us (23%)
  local copies, waits for them, and re-layouts  129 us (21%)
  other arithmetic  67.4 us (11%)
  matrix products  54.6 us (9%)
  between operations  28 us (5%)
  starting transfers between devices  7.54 us (1%)
    all_gather x1, waiting for transfers between devices, shards(): shard_rows = lax.all_gather(grad_pred, 'cell', axis=0, tiled=True)  125 us
    gather x1, local copies, waits for them, and re-layouts, shards(): spot_valid[clamped] == 1  60.4 us
    reduce_scatter x1, waiting for transfers between devices, shards(): lax.psum_scatter(lax.dot_general(columns, mapping, (((0,), (0,)), ((), ()...  44.7 us
    scatter-add x6, other arithmetic, shards(): spread = spread.at[:, position[:, k]].add(linked[:, k][None, :] * spread_in)  42.3 us
    psum x1, blocking collectives, shards(): lax.psum((first_spot * jnp.sum(cos_gene), first_cell * jnp.sum(valid_here...  39.3 us
    psum x1, blocking collectives, shards(): lax.psum((jnp.sum(smoothed * spatial, axis=0), jnp.sum(smoothed * smoothe...  35.2 us
    gather x2, local copies, waits for them, and re-layouts, shards(): slide_ids[clamped] == slide_here[:, None]  28.9 us
    gather x6, local copies, waits for them, and re-layouts, shards(): jnp.take(padded, position[:, k], axis=1)  28 us
  transfers between devices with their start and end apart: 8, of which 4 were waited for; matrix products, arithmetic and copies ran while one was open for 21% of the time, Pallas kernels for 0%

commit v1 on v0

--- a/solution.py
+++ b/solution.py
@@ -8,6 +8,18 @@
 SLIDES = 3
 epsilon = 1e-06
 highest = lax.Precision.HIGHEST
+
+
+def gather_by_bits(x, axis, dim):
+    ways, here = (lax.axis_size(axis), lax.axis_index(axis))
+    grown, reach = (x, 1)
+    while reach < ways:
+        theirs = lax.ppermute(grown, axis, [(d, d ^ reach) for d in range(ways)])
+        mine_first = jnp.concatenate([grown, theirs], axis=dim)
+        theirs_first = jnp.concatenate([theirs, grown], axis=dim)
+        grown = jnp.where(here & reach == 0, mine_first, theirs_first)
+        reach = 2 * reach
+    return grown
 
 
 def padded_2(shard, sides, width):
@@ -123,7 +135,7 @@
         grad_pred
         + (total_cells * total_spots * valid_here * (1.0 / slide_rows - target / row_sums))[None, :]
     )
-    shard_rows = lax.all_gather(grad_pred, "cell", axis=0, tiled=True)
+    shard_rows = gather_by_bits(grad_pred, "cell", 0)
     columns = genes_all
     grad_map = jnp.dot(columns, shard_rows, precision=highest)
     block_grad = lax.dot_general(mapping, shard_rows, (((1,), (1,)), ((), ())), precision=highest)

time: 610 us -> 749 us (1.23)
  waiting for transfers between devices: 174 us -> 305 us
    ppermute x0 -> x3, waiting for transfers between devices: none -> 256 us  [gather_by_bits(): theirs = lax.ppermute(grown, axis, [(d, d ^ reach) for d in range(ways)])]
    all_gather x1 -> x0, waiting for transfers between devices: 125 us -> none  [shards(): shard_rows = lax.all_gather(grad_pred, 'cell', axis=0, tiled=True)]
    select_n x0 -> x2, other arithmetic: none -> 8.23 us  [gather_by_bits(): grown = jnp.where(here & reach == 0, mine_first, theirs_first)]
  transfers between devices with their start and end apart: 8 -> 10, of which waited for: 4 -> 6; matrix products, arithmetic and copies ran while one was open for 21% -> 17% of each run, Pallas kernels for 0% -> 0%
where the time goes in v1:
time: 749 us; the launch traced here: 742 us
  waiting for transfers between devices  305 us (41%)
  blocking collectives  141 us (19%)
  local copies, waits for them, and re-layouts  129 us (17%)
  other arithmetic  73.6 us (10%)
  matrix products  58.6 us (8%)
  between operations  28 us (4%)
    ppermute x3, waiting for transfers between devices, gather_by_bits(): theirs = lax.ppermute(grown, axis, [(d, d ^ reach) for d in range(ways)])  256 us
    gather x1, local copies, waits for them, and re-layouts, shards(): spot_valid[clamped] == 1  60.4 us
    reduce_scatter x1, waiting for transfers between devices, shards(): lax.psum_scatter(lax.dot_general(columns, mapping, (((0,), (0,)), ((), ()...  44.6 us
    scatter-add x6, other arithmetic, shards(): spread = spread.at[:, position[:, k]].add(linked[:, k][None, :] * spread_in)  42.3 us
    psum x1, blocking collectives, shards(): lax.psum((first_spot * jnp.sum(cos_gene), first_cell * jnp.sum(valid_here...  37.7 us
    psum x1, blocking collectives, shards(): lax.psum((jnp.sum(smoothed * spatial, axis=0), jnp.sum(smoothed * smoothe...  35.2 us
    gather x2, local copies, waits for them, and re-layouts, shards(): slide_ids[clamped] == slide_here[:, None]  28.9 us
    gather x6, local copies, waits for them, and re-layouts, shards(): jnp.take(padded, position[:, k], axis=1)  28.1 us
  transfers between devices with their start and end apart: 10, of which 6 were waited for; matrix products, arithmetic and copies ran while one was open for 17% of the time, Pallas kernels for 0%

profile of v1, /device:TPU:0, one launch (start us, length us, event | category | flops | bytes accessed | tf_op | source)
XLA Modules:
  0.0 742.3 jit_solution(2370716538496674863)
XLA Ops:
  9.7 23.2 %pmax.7 = f32[1024]{0:T(1024)S(1)} all-reduce(f32[1024]{0:T(1024)S(1)} %reduce_max.9), channel_id=1, replica_groups=mesh['spot'=4,'cell'=8] {'cell'}, use_global_device_ids=true, to_apply=%region_1.0 | all-reduce | flops 1024 | bytes 8192 | tf_op jit(solution)/shard_map/pmax | solution.py:65
  33.2 17.1 %psum.119 = f32[1024]{0:T(1024)S(1)} all-reduce(f32[1024]{0:T(1024)S(1)} %fusion.7), channel_id=1, replica_groups=mesh['spot'=4,'cell'=8] {'cell'}, use_global_device_ids=true, to_apply=%region_3.4 | all-reduce | flops 1024 | bytes 8192 | tf_op jit(solution)/shard_map/psum | solution.py:67
  50.4 17.4 %convolution_bitcast_fusion = f32[2048,1024]{0,1:T(8,128)} fusion(f32[512,2048]{1,0:T(8,128)} %all-gather.2.cloned.1.call-done, f32[512,1024]{1,0:T(8,128)S(1)} %copy-done.3, f32[1024]{0:T(1024)S(1)} %psum.119, f32[1024]{0:T(1024)S(1)} %pmax.7), kind=kOutput, calls=%fused_computation.17 | convolution fusion | flops 12885950464 | bytes 14688256 | tf_op jit(solution)/shard_map/dot_general | solution.py:72
  72.4 60.4 %gather_fusion = s32[6144]{0:T(1024)} fusion(s32[4096]{0:T(1024)S(1)} %copy-done, s32[6144]{0:T(1024)S(1)} %broadcast_clamp_fusion), kind=kCustom, calls=%fused_computation.6 | custom fusion | bytes 73728 | tf_op jit(solution)/shard_map/gather | solution.py:57
  132.8 28.4 %gather_fusion.1 = s32[6144]{0:T(1024)S(1)} fusion(s32[4096]{0:T(1024)} %param.17, s32[6144]{0:T(1024)S(1)} %broadcast_clamp_fusion), kind=kCustom, calls=%fused_computation.7 | custom fusion | bytes 73728 | tf_op jit(solution)/shard_map/gather | solution.py:57
  169.9 44.6 %reduce-scatter.3.cloned.1.call-done = f32[256,1024]{0,1:T(8,128)} async-done(((f32[2048,1024]{0,1:T(8,128)}), f32[256,1024]{0,1:T(8,128)}) %reduce-scatter.3.cloned.1.call-update) | async-done | bytes 1048592 | tf_op jit(solution)/shard_map/reduce_scatter | solution.py:71
  229.5 4.7 gather_fusion.6
  253.0 7.7 %multiply_reduce_fusion.3 = (f32[1024]{0:T(1024)S(1)}, f32[256]{0:T(256)S(1)}, f32[]{:T(128)}, f32[256]{0:T(256)S(1)}, f32[256]{0:T(256)S(1)}, /*index=5*/f32[10...) fusion(f32[256,1024]{0,1:T(8,128)S(1)} %copy-done.6, f32[1024]{0:T(1024)S(1)} %get-tuple-element.85, ...), kind=kLoop, calls=%fused_computation.78 | loop fusion | flops 9433342 | bytes 9491464 | tf_op jit(solution)/shard_map/reduce_sum | solution.py:84
  260.6 35.2 %all-reduce.1 = (f32[1024]{0:T(1024)S(1)}, f32[1024]{0:T(1024)S(1)}, f32[1024]{0:T(1024)S(1)}, f32[1024]{0:T(1024)S(1)}) all-reduce(f32[1024]{0:T(1024)S(1)} %get-tuple-element.61, f32[1024]{0:T(1024)S(1)} %get-tuple-element.35, f32[1024]{0:T(1024)S(1)} %multiply_reduce_fusion.1, ...), channel_id=1, replica_groups=mesh['spot'=4,'cell'=8] {'cell'}, use_global_device_ids=true, to_apply=%region_27.29 | all-reduce | flops 4096 | bytes 32768 | tf_op jit(solution)/shard_map/psum | solution.py:82
  296.0 6.6 all-reduce.2
  304.9 6.8 scatter_custom_fusion
  311.7 7.0 scatter_custom_fusion.1
  318.7 7.1 scatter_custom_fusion.2
  325.8 7.1 scatter_custom_fusion.3
  332.8 7.4 scatter_custom_fusion.4
  340.2 7.0 scatter_custom_fusion.5
  354.2 24.8 %collective-permute-done.4 = f32[256,1024]{0,1:T(8,128)S(1)} collective-permute-done((f32[256,1024]{0,1:T(8,128)S(1)}, f32[256,1024]{0,1:T(8,128)S(1)}, u32[]{:S(2)}, u32[]{:S(2)}) %collective-permute-start.4) | collective-permute-done | bytes 1048608 | tf_op jit(solution)/shard_map/ppermute | solution.py:17
  380.7 48.8 %collective-permute-done.5 = f32[512,1024]{0,1:T(8,128)} collective-permute-done((f32[512,1024]{0,1:T(8,128)}, f32[512,1024]{0,1:T(8,128)}, u32[]{:S(2)}, u32[]{:S(2)}) %collective-permute-start.5) | collective-permute-done | bytes 2097184 | tf_op jit(solution)/shard_map/ppermute | solution.py:17
  429.5 6.6 maximum_select_fusion.3
  436.1 182.9 %collective-permute-done.6 = f32[1024,1024]{0,1:T(8,128)} collective-permute-done((f32[1024,1024]{0,1:T(8,128)}, f32[1024,1024]{0,1:T(8,128)}, u32[]{:S(2)}, u32[]{:S(2)}) %collective-permute-start.6) | collective-permute-done | bytes 4194336 | tf_op jit(solution)/shard_map/ppermute | solution.py:17
  618.9 19.6 %fusion = f32[512,2048]{1,0:T(8,128)} fusion(f32[1024,1024]{0,1:T(8,128)} %collective-permute-done.6, f32[1024,1024]{0,1:T(8,128)} %maximum_select_fusion.3, pred[]{:T(512)S(6)} %eq.51, f32[512,1024]{1,0:T(8,128)S(1)} %copy-done.4, f32[1024]{0:T(1024)S(1)} %copy-done.16, f32[1024]{0:T(1024)S(1)} %copy-done.13), kind=kOutput, calls=%fused_computation.15 | convolution fusion | flops 12892241920 | bytes 14688257 | tf_op jit(solution)/shard_map/dot_general | solution.py:141
  641.8 21.6 %multiply_reduce_fusion = (f32[]{:T(128)}, f32[1024]{0:T(1024)S(1)}, f32[1024,512]{0,1:T(8,128)}) fusion(f32[1024]{0:T(1024)S(1)} %get-tuple-element.85, f32[1024]{0:T(1024)S(1)} %copy-done.16, f32[512,1024]{1,0:T(8,128)S(1)} %copy-done.4, f32[1024]{0:T(1024)S(1)} %copy-done.13, f32[512,2048]{1,0:T(8,128)} %all-gather.2.cloned.1.call-done, ...), kind=kOutput, calls=%fused_computation.26 | convolution fusion | flops 12894862336 | bytes 16793604 | tf_op jit(solution)/shard_map/dot_general | solution.py:140
  663.4 37.7 %all-reduce = (f32[]{:T(128)}, f32[]{:T(128)}, f32[]{:T(128)}, f32[]{:T(128)}, f32[]{:T(128)}, /*index=5*/f32[]{:T(128)}) all-reduce(f32[]{:T(128)S(6)} %mul.342, f32[]{:T(128)S(6)} %mul.349, f32[]{:T(128)S(6)} %mul.362, f32[]{:T(128)} %get-tuple-element.33, ...), channel_id=1, replica_groups=mesh['spot'=4,'cell'=8] {'spot','cell'}, use_global_device_ids=true, to_apply=%region_13.15 | all-reduce | flops 6 | bytes 48 | tf_op jit(solution)/shard_map/psum | solution.py:149
  705.2 21.3 %psum.132 = f32[1024]{0:T(1024)S(1)} all-reduce(f32[1024]{0:T(1024)S(1)} %get-tuple-element.34), channel_id=1, replica_groups=mesh['spot'=4,'cell'=8] {'cell'}, use_global_device_ids=true, to_apply=%region_41.43 | all-reduce | flops 1024 | bytes 8192 | tf_op jit(solution)/shard_map/psum | solution.py:144
  (103 shorter events, 63.5 us)
Async XLA Ops:
  7.2 25.7 %copy-start.3 = (f32[512,1024]{1,0:T(8,128)S(1)}, f32[512,1024]{1,0:T(8,128)}, u32[]{:S(2)}) copy-start(f32[512,1024]{1,0:T(8,128)} %param.13) | copy-start | bytes 6291460
  7.2 43.2 %all-gather.2.cloned.1.call-start = ((), (), s32[]{:S(2)}) async-start(), calls=%async_computation.2 | async-start | bytes 5242880 | tf_op jit(solution)/shard_map/all_gather | solution.py:69
  7.9 206.6 %reduce-scatter.3.cloned.1.call-start = ((), (), s32[]{:S(2)}) async-start(), calls=%async_computation.3 | async-start | bytes 9437184 | tf_op jit(solution)/shard_map/reduce_scatter | solution.py:71
  32.9 34.9 %copy-start.12 = (f32[1024]{0:T(1024)}, f32[1024]{0:T(1024)S(1)}, u32[]{:S(2)}) copy-start(f32[1024]{0:T(1024)S(1)} %pmax.7) | copy-start | bytes 12292
  50.3 17.4 %copy-start.15 = (f32[1024]{0:T(1024)}, f32[1024]{0:T(1024)S(1)}, u32[]{:S(2)}) copy-start(f32[1024]{0:T(1024)S(1)} %psum.119) | copy-start | bytes 12292
  67.8 3.1 copy-start.10
  67.8 662.1 %reduce-scatter.5.cloned.1.call-start = ((), (), s32[]{:S(2)}) async-start(), calls=%async_computation.4 | async-start | bytes 5242880 | tf_op jit(solution)/shard_map/reduce_scatter | solution.py:146
  132.8 29.6 %copy-start.11 = (s32[1024,6]{0,1:T(8,128)S(1)}, s32[1024,6]{0,1:T(8,128)}, u32[]{:S(2)}) copy-start(s32[1024,6]{0,1:T(8,128)} %param.19) | copy-start | bytes 73732
  132.8 29.9 %copy-start.5 = (s32[6144]{0:T(1024)S(1)}, s32[6144]{0:T(1024)}, u32[]{:S(2)}) copy-start(s32[6144]{0:T(1024)} %gather_fusion) | copy-start | bytes 73732
  132.8 30.5 %copy-start.1 = (s32[4096]{0:T(1024)S(1)}, s32[4096]{0:T(1024)}, u32[]{:S(2)}) copy-start(s32[4096]{0:T(1024)} %param.18) | copy-start | bytes 49156
  132.8 32.5 %copy-start.9 = (f32[256,1024]{1,0:T(8,128)S(1)}, f32[256,1024]{1,0:T(8,128)}, u32[]{:S(2)}) copy-start(f32[256,1024]{1,0:T(8,128)} %param.15) | copy-start | bytes 3145732
  215.4 3.5 collective-permute-start
  216.9 4.7 collective-permute-start.1
  248.3 4.7 copy-start.6
  248.3 4.7 copy-start.7
  253.0 42.9 %copy-start.14 = (f32[1024]{0:T(1024)S(1)}, f32[1024]{0:T(1024)}, u32[]{:S(2)}) copy-start(f32[1024]{0:T(1024)} %param.16) | copy-start | bytes 12292
  347.2 4.5 collective-permute-start.2
  348.7 3.9 collective-permute-start.3
  354.1 24.9 %collective-permute-start.4 = (f32[256,1024]{0,1:T(8,128)S(1)}, f32[256,1024]{0,1:T(8,128)S(1)}, u32[]{:S(2)}, u32[]{:S(2)}) collective-permute-start(f32[256,1024]{0,1:T(8,128)S(1)} %broadcast_add_fusion), channel_id=1, source_target_pairs={{0,1},{1,0},{2,3},{3,2},{4,5},{5,4},{6,7},{7,6},{8,9},{9,8},{10,11... | collective-permute-start | bytes 3145736 | tf_op jit(solution)/shard_map/ppermute | solution.py:17
  380.7 48.8 %collective-permute-start.5 = (f32[512,1024]{0,1:T(8,128)}, f32[512,1024]{0,1:T(8,128)}, u32[]{:S(2)}, u32[]{:S(2)}) collective-permute-start(f32[512,1024]{0,1:T(8,128)} %maximum_select_fusion.4), channel_id=1, source_target_pairs={{0,2},{1,3},{2,0},{3,1},{4,6},{5,7},{6,4},{7,5},{8,10},{9,11},{10,... | collective-permute-start | bytes 6291464 | tf_op jit(solution)/shard_map/ppermute | solution.py:17
  380.7 238.2 %copy-start.4 = (f32[512,1024]{1,0:T(8,128)S(1)}, f32[512,1024]{1,0:T(8,128)}, u32[]{:S(2)}) copy-start(f32[512,1024]{1,0:T(8,128)} %param.13) | copy-start | bytes 6291460
  380.7 238.2 %copy-start.13 = (f32[1024]{0:T(1024)S(1)}, f32[1024]{0:T(1024)}, u32[]{:S(2)}) copy-start(f32[1024]{0:T(1024)} %copy-done.12) | copy-start | bytes 12292
  380.7 238.2 %copy-start.16 = (f32[1024]{0:T(1024)S(1)}, f32[1024]{0:T(1024)}, u32[]{:S(2)}) copy-start(f32[1024]{0:T(1024)} %copy-done.15) | copy-start | bytes 12292
  436.0 182.9 %collective-permute-start.6 = (f32[1024,1024]{0,1:T(8,128)}, f32[1024,1024]{0,1:T(8,128)}, u32[]{:S(2)}, u32[]{:S(2)}) collective-permute-start(f32[1024,1024]{0,1:T(8,128)} %maximum_select_fusion.3), channel_id=1, source_target_pairs={{0,4},{1,5},{2,6},{3,7},{4,0},{5,1},{6,2},{7,3},{8,12},{9,13},{10,... | collective-permute-start | bytes 12582920 | tf_op jit(solution)/shard_map/ppermute | solution.py:17
  (3 other events, 5.7 us)
Sparse Core Ops, SparseCore 0:
  9.5 37.1 all-gather.1
  67.9 146.5 reduce-scatter.2
  638.7 41.4 reduce-scatter.4
